TPU v7x, 32 devices: a whole 2x2x4 slice. The times are simulated.
32 devices in a mesh: dp: 4 (over y, x), hidden: 8 (over z, core).
Axes of the slice: x: 2, y: 2, z: 4, core: 2. Of those that a mesh axis runs over, the one named last changes fastest.
Arguments:
- tokens: bfloat16 [2048, 6144], P('dp', 'hidden'), as said below
- cotangent: bfloat16 [2048, 6144], P('dp', 'hidden'), may hold values from -6 to 6
- weight_in: bfloat16 [6144, 3072], P('hidden'), may hold values from -0.21875 to 0.21875
- level_weights: bfloat16 [3, 192, 2, 128, 128], P(None, 'hidden'), may hold values from -0.375 to 0.375
- weight_out: bfloat16 [24576, 768], P('hidden'), may hold values from -0.109375 to 0.109375
- block_order: int32 [3, 24], replicated, may hold values from 0 to 23, each once within a row
Outputs:
- branch_output: bfloat16 [2048, 6144], P('dp', 'hidden')
- token_grad: bfloat16 [2048, 6144], P('dp', 'hidden')
- level_grad: float32 [3, 192, 2, 128, 128], P(None, 'hidden', None, 'dp')
- input_grad: float32 [6144, 3072], P(('hidden', 'dp'))
- output_grad: float32 [24576, 768], P(('hidden', 'dp'))
Inputs may be any that keep to these rules, and one draw needn't show every extreme that they name: Each row of block_order lists every number from 0 to 23 once. `tokens`: entries are finite.
All inputs are finite; a program needn't handle non-finite values.
Results may differ from a plain program's by a relative error of at most 0.017.
Values may be sent and summed in bfloat16 or wider, within the bound.
A program may use at most 192 MiB of HBM per device.

v0:
```python
import math

import jax
import jax.numpy as jnp
from jax import lax
from jax.sharding import PartitionSpec as P


def partner(value, axis, distance):
    mask = 2**distance
    pairs = [(source, source ^ mask) for source in range(lax.axis_size(axis))]
    return lax.ppermute(value, axis, pairs)


def local(tokens, cotangent, weight_in, level_weights, weight_out, block_order):
    wide = jnp.float32
    row_count, width_local = tokens.shape
    level_count, group_count = block_order.shape
    block_size = level_weights.shape[-1]
    feature_total = width_local * lax.axis_size("hidden")
    grad_scale = 1.0 / math.sqrt(row_count * lax.axis_size("dp"))
    tokens_wide = tokens.astype(wide)
    sum_squares = lax.psum(jnp.sum(tokens_wide * tokens_wide, axis=1), "hidden")
    recip_rms = lax.rsqrt(sum_squares / feature_total + 1e-06)[:, None]
    normed = (tokens_wide * recip_rms).astype(jnp.bfloat16)
    current = jnp.dot(normed, weight_in, preferred_element_type=wide).astype(jnp.bfloat16)
    current = current.reshape(row_count, group_count, block_size)
    positions = jnp.broadcast_to(
        jnp.arange(group_count, dtype=jnp.int32), (level_count, group_count)
    )
    inverse = (
        jnp.zeros_like(block_order).at[jnp.arange(level_count)[:, None], block_order].set(positions)
    )
    inputs_kept = []
    partner_kept = []
    for level_index in range(level_count):
        weights_now = level_weights[level_index]
        arrived = partner(current, "hidden", level_index)
        shifted = jnp.take(arrived, block_order[level_index], axis=1)
        mixed_out = jnp.einsum(
            "rjc,jcd->rjd", current, weights_now[:, 0], preferred_element_type=wide
        )
        mixed_out = mixed_out + jnp.einsum(
            "rjc,jcd->rjd", shifted, weights_now[:, 1], preferred_element_type=wide
        )
        inputs_kept.append(current)
        partner_kept.append(shifted)
        current = mixed_out.astype(jnp.bfloat16)
    top_layer = current.reshape(row_count, group_count * block_size).astype(wide)
    activated = jax.nn.gelu(top_layer).astype(jnp.bfloat16)
    result_out = jnp.dot(activated, weight_out, preferred_element_type=wide).astype(jnp.bfloat16)
    last_grad = (
        jnp.einsum("rf,rd->fd", activated, cotangent, preferred_element_type=wide) * grad_scale
    )
    d_hidden = jnp.einsum("rd,fd->rf", cotangent, weight_out, preferred_element_type=wide)
    _, pullback = jax.vjp(jax.nn.gelu, top_layer)
    upstream = (
        pullback(d_hidden)[0].astype(jnp.bfloat16).reshape(row_count, group_count, block_size)
    )
    level_list = [None] * level_count
    for level_index in reversed(range(level_count)):
        weights_now = level_weights[level_index]
        shifted = partner_kept[level_index]
        grad_own = jnp.einsum(
            "rjc,rjd->jcd", inputs_kept[level_index], upstream, preferred_element_type=wide
        )
        grad_partner = jnp.einsum("rjc,rjd->jcd", shifted, upstream, preferred_element_type=wide)
        stacked = jnp.stack([grad_own, grad_partner], axis=1) * grad_scale
        level_list[level_index] = stacked
        own_term = jnp.einsum(
            "rjd,jcd->rjc", upstream, weights_now[:, 0], preferred_element_type=wide
        )
        sent_term = jnp.einsum(
            "rjd,jcd->rjc", upstream, weights_now[:, 1], preferred_element_type=wide
        ).astype(jnp.bfloat16)
        returned = partner(sent_term, "hidden", level_index)
        placed = jnp.take(returned, inverse[level_index], axis=1)
        upstream = (own_term + placed.astype(wide)).astype(jnp.bfloat16)
    flat_grad = upstream.reshape(row_count, group_count * block_size)
    first_grad = (
        jnp.einsum("rc,rf->cf", normed, flat_grad, preferred_element_type=wide) * grad_scale
    )
    d_normed = jnp.einsum("rf,cf->rc", flat_grad, weight_in, preferred_element_type=wide)
    inner_sum = lax.psum(jnp.sum(d_normed * tokens_wide, axis=1), "hidden")
    inner_mean = (inner_sum / feature_total)[:, None]
    token_out = (
        recip_rms * d_normed - tokens_wide * recip_rms * recip_rms * recip_rms * inner_mean
    ).astype(jnp.bfloat16)
    level_stack = jnp.stack(level_list)
    level_stack, first_grad, last_grad = (
        lax.psum_scatter(level_stack, "dp", scatter_dimension=3, tiled=True),
        lax.psum_scatter(first_grad, "dp", scatter_dimension=0, tiled=True),
        lax.psum_scatter(last_grad, "dp", scatter_dimension=0, tiled=True),
    )
    return (result_out, token_out, level_stack, first_grad, last_grad)


def solution(mesh):
    in_specs = (
        P("dp", "hidden"),
        P("dp", "hidden"),
        P("hidden", None),
        P(None, "hidden", None, None, None),
        P("hidden", None),
        P(),
    )
    out_specs = (
        P("dp", "hidden"),
        P("dp", "hidden"),
        P(None, "hidden", None, "dp", None),
        P(("hidden", "dp"), None),
        P(("hidden", "dp"), None),
    )
    return jax.shard_map(local, mesh=mesh, in_specs=in_specs, out_specs=out_specs, check_vma=False)
```

profile of v0, /device:TPU:0, one launch (start us, length us, event | category | flops | bytes accessed | tf_op | source)
XLA Modules:
  0.0 834.5 jit_solution(11112016924307734944)
XLA Ops:
  8.7 18.1 %psum.14 = f32[512]{0:T(512)S(1)} all-reduce(f32[512]{0:T(512)S(1)} %fusion.52), channel_id=1, replica_groups=mesh['dp'=4,'hidden'=8] {'hidden'}, use_global_device_ids=true, to_apply=%region_1.0 | all-reduce | flops 512 | bytes 4096 | tf_op jit(solution)/shard_map/psum | solution.py:23
  26.8 5.4 fusion.45
  40.4 4.6 gather_fusion
  45.0 4.9 fusion.10
  54.1 66.4 %collective-permute-done.1 = bf16[512,24,128]{2,0,1:T(8,128)(2,1)} collective-permute-done((bf16[512,24,128]{2,0,1:T(8,128)(2,1)S(1)}, bf16[512,24,128]{2,0,1:T(8,128)(2,1)}, u32[]{:S(2)}, u32[]{:S(2)}) %collective-permute-start.1) | collective-permute-done | bytes 3145760 | tf_op jit(solution)/shard_map/ppermute | solution.py:12
  120.5 4.6 gather_fusion.1
  125.1 6.5 fusion.11
  133.6 5.5 fusion.70
  139.1 130.7 %collective-permute-done.2 = bf16[512,24,128]{2,0,1:T(8,128)(2,1)} collective-permute-done((bf16[512,24,128]{2,0,1:T(8,128)(2,1)}, bf16[512,24,128]{2,0,1:T(8,128)(2,1)}, u32[]{:S(2)}, u32[]{:S(2)}) %collective-permute-start.2) | collective-permute-done | bytes 3145760 | tf_op jit(solution)/shard_map/ppermute | solution.py:12
  269.8 4.6 gather_fusion.2
  274.5 7.5 fusion.12
  281.9 6.8 copy.43
  288.7 8.7 %fusion.32 = bf16[64,24,8,128]{3,2,1,0:T(8,128)(2,1)S(1)} fusion(f32[512,3072]{1,0:T(8,128)} %copy.43, bf16[512,768]{1,0:T(8,128)(2,1)S(1)} %copy-done, bf16[3072,768]{1,0:T(8,128)(2,1)} %param.12), kind=kOutput, calls=%fused_computation.62 | convolution fusion | flops 2447376384 | bytes 14942208 | tf_op jit(solution)/shard_map/rd,fd->rf/dot_general | solution.py:55
  300.2 4.2 scatter_fusion
  304.5 5.5 fusion.19
  310.0 125.6 %collective-permute-done.3 = bf16[512,24,128]{2,0,1:T(8,128)(2,1)} collective-permute-done((bf16[512,24,128]{2,0,1:T(8,128)(2,1)}, bf16[512,24,128]{2,0,1:T(8,128)(2,1)}, u32[]{:S(2)}, u32[]{:S(2)}) %collective-permute-start.3) | collective-permute-done | bytes 3145760 | tf_op jit(solution)/shard_map/ppermute | solution.py:12
  435.6 4.6 gather_fusion.3
  440.2 4.9 fusion.9
  461.1 55.2 %collective-permute-done.4 = bf16[512,24,128]{2,0,1:T(8,128)(2,1)} collective-permute-done((bf16[512,24,128]{2,0,1:T(8,128)(2,1)S(1)}, bf16[512,24,128]{2,0,1:T(8,128)(2,1)}, u32[]{:S(2)}, u32[]{:S(2)}) %collective-permute-start.4) | collective-permute-done | bytes 3145760 | tf_op jit(solution)/shard_map/ppermute | solution.py:12
  516.3 4.6 gather_fusion.4
  532.3 4.4 pad_maximum_fusion
  536.8 9.8 %convolution_multiply_fusion = f32[3072,768]{1,0:T(8,128)} fusion(bf16[512,768]{1,0:T(8,128)(2,1)S(1)} %copy-done, f32[512,3072]{1,0:T(8,128)} %copy.43), kind=kOutput, calls=%fused_computation.27 | convolution fusion | flops 2432434176 | bytes 16515072 | tf_op jit(solution)/shard_map/rf,rd->fd/dot_general | solution.py:53
  551.3 5.8 collective-permute-done.5
  557.1 4.7 gather_fusion.5
  561.8 5.0 copy.49
  572.7 5.5 convolution_multiply_fusion.1
  578.2 9.2 %convolution_convert_fusion.1 = bf16[512,768]{1,0:T(8,128)(2,1)} fusion(bf16[3072,768]{1,0:T(8,128)(2,1)} %param.12, f32[512,3072]{1,0:T(8,128)} %copy.43), kind=kOutput, calls=%fused_computation.87 | convolution fusion | flops 2430468096 | bytes 11796480 | tf_op jit(solution)/shard_map/dot_general | solution.py:51
  587.4 5.2 fusion.53
  592.6 14.0 %psum.15 = f32[512]{0:T(512)S(1)} all-reduce(f32[512]{0:T(512)S(1)} %get-tuple-element.39), channel_id=1, replica_groups=mesh['dp'=4,'hidden'=8] {'hidden'}, use_global_device_ids=true, to_apply=%region_4.6 | all-reduce | flops 512 | bytes 4096 | tf_op jit(solution)/shard_map/psum | solution.py:84
  607.9 22.7 %reduce-scatter.4.cloned.1.call-done = f32[3,24,2,32,128]{4,3,1,2,0:T(8,128)} async-done(((f32[3,24,2,128,128]{4,3,1,2,0:T(8,128)}), f32[3,24,2,32,128]{4,3,1,2,0:T(8,128)}) %reduce-scatter.4.cloned.1.call-update) | async-done | bytes 2359312 | tf_op jit(solution)/shard_map/reduce_scatter | solution.py:91
  633.9 95.3 %reduce-scatter.8.cloned.1.call-done = f32[768,768]{1,0:T(8,128)} async-done(((f32[3072,768]{1,0:T(8,128)}), f32[768,768]{1,0:T(8,128)}) %reduce-scatter.8.cloned.1.call-update) | async-done | bytes 2359312 | tf_op jit(solution)/shard_map/reduce_scatter | solution.py:93
  729.2 98.6 %reduce-scatter.6.cloned.1.call-done = f32[192,3072]{1,0:T(8,128)} async-done(((f32[768,3072]{1,0:T(8,128)}), f32[192,3072]{1,0:T(8,128)}) %reduce-scatter.6.cloned.1.call-update) | async-done | bytes 2359312 | tf_op jit(solution)/shard_map/reduce_scatter | solution.py:92
  (103 shorter events, 61.2 us)
Async XLA Ops:
  7.2 281.6 %copy-start = (bf16[512,768]{1,0:T(8,128)(2,1)S(1)}, bf16[512,768]{1,0:T(8,128)(2,1)}, u32[]{:S(2)}) copy-start(bf16[512,768]{1,0:T(8,128)(2,1)} %param.9) | copy-start | bytes 2359300
  7.2 623.4 %reduce-scatter.4.cloned.1.call-start = ((), (), s32[]{:S(2)}) async-start(), calls=%async_computation.3 | async-start | bytes 11796480 | tf_op jit(solution)/shard_map/reduce_scatter | solution.py:91
  26.8 6.4 slice-start
  26.8 6.4 slice-start.1
  32.2 4.6 copy-start.4
  33.1 7.3 collective-permute-start
  36.7 8.3 copy-start.14
  45.0 5.0 copy-start.18
  49.9 4.2 copy-start.6
  49.9 70.6 %collective-permute-start.1 = (bf16[512,24,128]{2,0,1:T(8,128)(2,1)S(1)}, bf16[512,24,128]{2,0,1:T(8,128)(2,1)}, u32[]{:S(2)}, u32[]{:S(2)}) collective-permute-start(bf16[512,24,128]{2,0,1:T(8,128)(2,1)S(1)} %fusion.10), channel_id=1, source_target_pairs={{0,2},{1,3},{2,0},{3,1},{4,6},{5,7},{6,4},{7,5},{8,10},{9,11},{10,... | collective-permute-start | bytes 9437192 | tf_op jit(solution)/shard_map/ppermute | solution.py:12
  50.1 75.0 %copy-start.16 = (bf16[1,24,2,128,128]{4,3,1,2,0:T(8,128)(2,1)}, bf16[1,24,2,128,128]{4,3,1,2,0:T(8,128)(2,1)S(1)}, u32[]{:S(2)}) copy-start(bf16[1,24,2,128,128]{4,3,1,2,0:T(8,128)(2,1)S(1)} %copy.97) | copy-start | bytes 4718596
  131.6 138.2 %collective-permute-start.2 = (bf16[512,24,128]{2,0,1:T(8,128)(2,1)}, bf16[512,24,128]{2,0,1:T(8,128)(2,1)}, u32[]{:S(2)}, u32[]{:S(2)}) collective-permute-start(bf16[512,24,128]{2,0,1:T(8,128)(2,1)} %fusion.11), channel_id=1, source_target_pairs={{0,4},{1,5},{2,6},{3,7},{4,0},{5,1},{6,2},{7,3},{8,12},{9,13},{10,... | collective-permute-start | bytes 9437192 | tf_op jit(solution)/shard_map/ppermute | solution.py:12
  297.4 2.7 copy-start.1
  300.1 135.6 %collective-permute-start.3 = (bf16[512,24,128]{2,0,1:T(8,128)(2,1)}, bf16[512,24,128]{2,0,1:T(8,128)(2,1)}, u32[]{:S(2)}, u32[]{:S(2)}) collective-permute-start(bf16[512,24,128]{2,0,1:T(8,128)(2,1)} %convert_bitcast_fusion.2), channel_id=1, source_target_pairs={{0,4},{1,5},{2,6},{3,7},{4,0},{5,1},{6,2},{7,3},{8,12},{9,13},{10,... | collective-permute-start | bytes 9437192 | tf_op jit(solution)/shard_map/ppermute | solution.py:12
  440.2 4.9 copy-start.17
  445.1 11.8 %copy-start.3 = (bf16[512,24,128]{2,0,1:T(8,128)(2,1)}, bf16[512,24,128]{2,0,1:T(8,128)(2,1)S(1)}, u32[]{:S(2)}) copy-start(bf16[512,24,128]{2,0,1:T(8,128)(2,1)S(1)} %fusion.9) | copy-start | bytes 9437188
  445.1 3.0 copy-start.2
  446.1 70.2 %collective-permute-start.4 = (bf16[512,24,128]{2,0,1:T(8,128)(2,1)S(1)}, bf16[512,24,128]{2,0,1:T(8,128)(2,1)}, u32[]{:S(2)}, u32[]{:S(2)}) collective-permute-start(bf16[512,24,128]{2,0,1:T(8,128)(2,1)S(1)} %convert_bitcast_fusion.1), channel_id=1, source_target_pairs={{0,2},{1,3},{2,0},{3,1},{4,6},{5,7},{6,4},{7,5},{8,10},{9,11},{10,... | collective-permute-start | bytes 9437192 | tf_op jit(solution)/shard_map/ppermute | solution.py:12
  448.2 3.3 copy-start.8
  452.9 3.0 copy-start.7
  455.9 1.9 copy-start.13
  520.9 4.0 copy-start.12
  524.9 1.7 copy-start.11
  524.9 3.0 copy-start.5
  529.5 1.9 copy-start.9
  529.5 2.8 copy-start.10
  536.7 192.4 %reduce-scatter.8.cloned.1.call-start = ((), (), s32[]{:S(2)}) async-start(), calls=%async_computation.5 | async-start | bytes 11796480 | tf_op jit(solution)/shard_map/reduce_scatter | solution.py:93
  546.6 281.1 %reduce-scatter.6.cloned.1.call-start = ((), (), s32[]{:S(2)}) async-start(), calls=%async_computation.4 | async-start | bytes 11796480 | tf_op jit(solution)/shard_map/reduce_scatter | solution.py:92
  551.2 5.9 collective-permute-start.5
  566.8 5.9 copy-start.19
  571.0 1.7 copy-start.21
  578.2 9.2 %copy-start.22 = (bf16[512,24,128]{0,2,1:T(8,128)(2,1)S(1)}, bf16[512,24,128]{0,2,1:T(8,128)(2,1)}, u32[]{:S(2)}) copy-start(bf16[512,24,128]{0,2,1:T(8,128)(2,1)} %copy-done.21) | copy-start | bytes 9437188
  (2 other events, 2.1 us)
Sparse Core Ops, SparseCore 0:
  536.9 93.6 reduce-scatter.3
  634.2 94.8 reduce-scatter.7
  732.8 94.8 reduce-scatter.5
where the time goes:
time: 850 us; the launch traced here: 835 us
  waiting for transfers between devices  600 us (71%)
  matrix products  106 us (12%)
  local copies, waits for them, and re-layouts  64.9 us (8%)
  blocking collectives  32.1 us (4%)
  other arithmetic  16.5 us (2%)
  between operations  14.4 us (2%)
    ppermute x6, waiting for transfers between devices, partner(): return lax.ppermute(value, axis, pairs)  384 us
    reduce_scatter x1, waiting for transfers between devices, local(): lax.psum_scatter(first_grad, 'dp', scatter_dimension=0, tiled=True)  98.6 us
    reduce_scatter x1, waiting for transfers between devices, local(): lax.psum_scatter(last_grad, 'dp', scatter_dimension=0, tiled=True)  95.3 us
    reduce_scatter x1, waiting for transfers between devices, local(): lax.psum_scatter(level_stack, 'dp', scatter_dimension=3, tiled=True)  22.7 us
    gather x4, local copies, waits for them, and re-layouts, local(): placed = jnp.take(returned, inverse[level_index], axis=1)  18.9 us
    dot_general x3, matrix products, local(): jnp.einsum('rjc,jcd->rjd', shifted, weights_now[:, 1], preferred_element_...  18.8 us
    psum x1, blocking collectives, local(): sum_squares = lax.psum(jnp.sum(tokens_wide * tokens_wide, axis=1), 'hidden')  18.1 us
    unnamed x54, local copies, waits for them, and re-layouts  17.4 us
  transfers between devices with their start and end apart: 9, of which 8 were waited for; matrix products, arithmetic and copies ran while one was open for 11% of the time, Pallas kernels for 0%

commit v1 on v0

--- a/solution.py
+++ b/solution.py
@@ -10,6 +10,11 @@
     mask = 2**distance
     pairs = [(source, source ^ mask) for source in range(lax.axis_size(axis))]
     return lax.ppermute(value, axis, pairs)
+
+
+def reduce_dp(value, dim, scale):
+    summed = lax.psum_scatter(value.astype(jnp.bfloat16), "dp", scatter_dimension=dim, tiled=True)
+    return summed.astype(jnp.float32) * scale
 
 
 def local(tokens, cotangent, weight_in, level_weights, weight_out, block_order):
@@ -49,8 +54,8 @@
     top_layer = current.reshape(row_count, group_count * block_size).astype(wide)
     activated = jax.nn.gelu(top_layer).astype(jnp.bfloat16)
     result_out = jnp.dot(activated, weight_out, preferred_element_type=wide).astype(jnp.bfloat16)
-    last_grad = (
-        jnp.einsum("rf,rd->fd", activated, cotangent, preferred_element_type=wide) * grad_scale
+    last_grad = reduce_dp(
+        jnp.einsum("rf,rd->fd", activated, cotangent, preferred_element_type=wide), 0, grad_scale
     )
     d_hidden = jnp.einsum("rd,fd->rf", cotangent, weight_out, preferred_element_type=wide)
     _, pullback = jax.vjp(jax.nn.gelu, top_layer)
@@ -65,8 +70,8 @@
             "rjc,rjd->jcd", inputs_kept[level_index], upstream, preferred_element_type=wide
         )
         grad_partner = jnp.einsum("rjc,rjd->jcd", shifted, upstream, preferred_element_type=wide)
-        stacked = jnp.stack([grad_own, grad_partner], axis=1) * grad_scale
-        level_list[level_index] = stacked
+        stacked = jnp.stack([grad_own, grad_partner], axis=1)
+        level_list[level_index] = reduce_dp(stacked, 2, grad_scale)
         own_term = jnp.einsum(
             "rjd,jcd->rjc", upstream, weights_now[:, 0], preferred_element_type=wide
         )
@@ -77,8 +82,8 @@
         placed = jnp.take(returned, inverse[level_index], axis=1)
         upstream = (own_term + placed.astype(wide)).astype(jnp.bfloat16)
     flat_grad = upstream.reshape(row_count, group_count * block_size)
-    first_grad = (
-        jnp.einsum("rc,rf->cf", normed, flat_grad, preferred_element_type=wide) * grad_scale
+    first_grad = reduce_dp(
+        jnp.einsum("rc,rf->cf", normed, flat_grad, preferred_element_type=wide), 0, grad_scale
     )
     d_normed = jnp.einsum("rf,cf->rc", flat_grad, weight_in, preferred_element_type=wide)
     inner_sum = lax.psum(jnp.sum(d_normed * tokens_wide, axis=1), "hidden")
@@ -87,11 +92,6 @@
         recip_rms * d_normed - tokens_wide * recip_rms * recip_rms * recip_rms * inner_mean
     ).astype(jnp.bfloat16)
     level_stack = jnp.stack(level_list)
-    level_stack, first_grad, last_grad = (
-        lax.psum_scatter(level_stack, "dp", scatter_dimension=3, tiled=True),
-        lax.psum_scatter(first_grad, "dp", scatter_dimension=0, tiled=True),
-        lax.psum_scatter(last_grad, "dp", scatter_dimension=0, tiled=True),
-    )
     return (result_out, token_out, level_stack, first_grad, last_grad)
 
 

time: 850 us -> 702 us (0.83)
  waiting for transfers between devices: 600 us -> 458 us
    reduce_scatter x3 -> x5, waiting for transfers between devices: 217 us -> 72 us  [reduce_dp(): lax.psum_scatter(value.astype(jnp.bfloat16), 'dp', scatter_dimension=dim,...]
    unnamed x54 -> x50, local copies, waits for them, and re-layouts: 17.4 us -> 12.4 us
  transfers between devices with their start and end apart: 9 -> 11, of which waited for: 8 -> 7; matrix products, arithmetic and copies ran while one was open for 11% -> 17% of each run, Pallas kernels for 0% -> 0%
where the time goes in v1:
time: 702 us; the launch traced here: 692 us
  waiting for transfers between devices  458 us (65%)
  matrix products  106 us (15%)
  local copies, waits for them, and re-layouts  59.6 us (8%)
  blocking collectives  31.8 us (5%)
  other arithmetic  21 us (3%)
  between operations  14.4 us (2%)
    ppermute x6, waiting for transfers between devices, partner(): return lax.ppermute(value, axis, pairs)  386 us
    reduce_scatter x5, waiting for transfers between devices, reduce_dp(): lax.psum_scatter(value.astype(jnp.bfloat16), 'dp', scatter_dimension=dim,...  72 us
    dot_general x3, matrix products, local(): jnp.einsum('rjc,jcd->rjd', shifted, weights_now[:, 1], preferred_element_...  18.9 us
    gather x4, local copies, waits for them, and re-layouts, local(): placed = jnp.take(returned, inverse[level_index], axis=1)  18.4 us
    psum x1, blocking collectives, local(): sum_squares = lax.psum(jnp.sum(tokens_wide * tokens_wide, axis=1), 'hidden')  18.1 us
  transfers between devices with their start and end apart: 11, of which 7 were waited for; matrix products, arithmetic and copies ran while one was open for 17% of the time, Pallas kernels for 0%

profile of v1, /device:TPU:0, one launch (start us, length us, event | category | flops | bytes accessed | tf_op | source)
XLA Modules:
  0.0 691.7 jit_solution(6938422605933272637)
XLA Ops:
  8.7 18.1 %psum.14 = f32[512]{0:T(512)S(1)} all-reduce(f32[512]{0:T(512)S(1)} %fusion.52), channel_id=1, replica_groups=mesh['dp'=4,'hidden'=8] {'hidden'}, use_global_device_ids=true, to_apply=%region_1.0 | all-reduce | flops 512 | bytes 4096 | tf_op jit(solution)/shard_map/psum | solution.py:28
  26.8 5.4 fusion.45
  40.3 4.6 gather_fusion
  45.0 4.9 fusion.10
  54.0 66.5 %collective-permute-done.1 = bf16[512,24,128]{2,0,1:T(8,128)(2,1)} collective-permute-done((bf16[512,24,128]{2,0,1:T(8,128)(2,1)S(1)}, bf16[512,24,128]{2,0,1:T(8,128)(2,1)}, u32[]{:S(2)}, u32[]{:S(2)}) %collective-permute-start.1) | collective-permute-done | bytes 3145760 | tf_op jit(solution)/shard_map/ppermute | solution.py:12
  120.5 4.6 gather_fusion.1
  125.1 6.5 fusion.11
  133.6 5.6 fusion.86
  139.1 130.7 %collective-permute-done.2 = bf16[512,24,128]{2,0,1:T(8,128)(2,1)} collective-permute-done((bf16[512,24,128]{2,0,1:T(8,128)(2,1)}, bf16[512,24,128]{2,0,1:T(8,128)(2,1)}, u32[]{:S(2)}, u32[]{:S(2)}) %collective-permute-start.2) | collective-permute-done | bytes 3145760 | tf_op jit(solution)/shard_map/ppermute | solution.py:12
  269.8 4.6 gather_fusion.2
  274.5 7.5 %fusion.12 = f32[24,512,128]{1,2,0:T(8,128)} fusion(f32[24,512,128]{1,2,0:T(8,128)} %fusion.86, bf16[24,512,128]{2,1,0:T(8,128)(2,1)} %gather_fusion.2, pred[24]{0:T(512)(128)(4,1)S(1)} %get-tuple-element.22, bf16[24,2,128,128]{2,3,0,1:T(8,128)(2,1)S(1)} %bitcast.189), kind=kOutput, calls=%fused_computation.31 | convolution fusion | flops 408944640 | bytes 16515584 | tf_op jit(solution)/shard_map/rjc,jcd->rjd/dot_general | solution.py:48
  282.0 6.7 copy.43
  288.7 8.7 %fusion.32 = bf16[64,24,8,128]{3,2,1,0:T(8,128)(2,1)S(1)} fusion(f32[512,3072]{1,0:T(8,128)} %copy.43, bf16[512,768]{1,0:T(8,128)(2,1)S(1)} %copy-done, bf16[3072,768]{1,0:T(8,128)(2,1)} %param.12), kind=kOutput, calls=%fused_computation.58 | convolution fusion | flops 2447376384 | bytes 14942208 | tf_op jit(solution)/shard_map/rd,fd->rf/dot_general | solution.py:60
  300.3 4.2 scatter_fusion
  304.5 4.2 fusion.73
  312.4 5.5 fusion.19
  317.9 117.8 %collective-permute-done.3 = bf16[512,24,128]{2,0,1:T(8,128)(2,1)} collective-permute-done((bf16[512,24,128]{2,0,1:T(8,128)(2,1)}, bf16[512,24,128]{2,0,1:T(8,128)(2,1)}, u32[]{:S(2)}, u32[]{:S(2)}) %collective-permute-start.3) | collective-permute-done | bytes 3145760 | tf_op jit(solution)/shard_map/ppermute | solution.py:12
  435.7 4.6 gather_fusion.3
  440.3 4.9 fusion.9
  453.1 65.1 %collective-permute-done.4 = bf16[512,24,128]{2,0,1:T(8,128)(2,1)} collective-permute-done((bf16[512,24,128]{2,0,1:T(8,128)(2,1)}, bf16[512,24,128]{2,0,1:T(8,128)(2,1)}, u32[]{:S(2)}, u32[]{:S(2)}) %collective-permute-start.4) | collective-permute-done | bytes 3145760 | tf_op jit(solution)/shard_map/ppermute | solution.py:12
  518.2 4.6 gather_fusion.4
  532.4 8.2 %convolution_convert_fusion = bf16[3072,768]{1,0:T(8,128)(2,1)} fusion(bf16[512,768]{1,0:T(8,128)(2,1)S(1)} %copy-done, f32[512,3072]{1,0:T(8,128)} %copy.43), kind=kOutput, calls=%fused_computation.26 | convolution fusion | flops 2432434176 | bytes 11796480 | tf_op jit(solution)/shard_map/rf,rd->fd/dot_general | solution.py:58
  545.1 5.8 collective-permute-done.5
  550.9 4.6 gather_fusion.5
  555.5 4.6 copy.49
  560.1 4.0 fusion.7
  565.8 4.8 convolution_convert_fusion.1
  570.6 9.5 %convolution_convert_fusion.5 = bf16[512,768]{1,0:T(8,128)(2,1)} fusion(bf16[3072,768]{1,0:T(8,128)(2,1)} %param.12, f32[512,3072]{1,0:T(8,128)} %copy.43), kind=kOutput, calls=%fused_computation.89 | convolution fusion | flops 2430468096 | bytes 11796480 | tf_op jit(solution)/shard_map/dot_general | solution.py:56
  586.7 5.5 fusion.53
  592.1 13.7 %psum.15 = f32[512]{0:T(512)S(1)} all-reduce(f32[512]{0:T(512)S(1)} %get-tuple-element.39), channel_id=1, replica_groups=mesh['dp'=4,'hidden'=8] {'hidden'}, use_global_device_ids=true, to_apply=%region_4.6 | all-reduce | flops 512 | bytes 4096 | tf_op jit(solution)/shard_map/psum | solution.py:89
  607.2 15.0 %reduce-scatter.14.cloned.1.call-done = bf16[768,768]{1,0:T(8,128)(2,1)} async-done(((bf16[3072,768]{1,0:T(8,128)(2,1)}), bf16[768,768]{1,0:T(8,128)(2,1)}) %reduce-scatter.14.cloned.1.call-update) | async-done | bytes 1179664 | tf_op jit(solution)/shard_map/reduce_scatter | solution.py:16
  625.1 56.9 %reduce-scatter.12.cloned.1.call-done = bf16[192,3072]{1,0:T(8,128)(2,1)} async-done(((bf16[768,3072]{1,0:T(8,128)(2,1)}), bf16[192,3072]{1,0:T(8,128)(2,1)}) %reduce-scatter.12.cloned.1.call-update) | async-done | bytes 1179664 | tf_op jit(solution)/shard_map/reduce_scatter | solution.py:16
  (110 shorter events, 59.3 us)
Async XLA Ops:
  7.2 281.6 %copy-start = (bf16[512,768]{1,0:T(8,128)(2,1)S(1)}, bf16[512,768]{1,0:T(8,128)(2,1)}, u32[]{:S(2)}) copy-start(bf16[512,768]{1,0:T(8,128)(2,1)} %param.9) | copy-start | bytes 2359300
  7.2 573.0 %reduce-scatter.10.cloned.1.call-start = ((), (), s32[]{:S(2)}) async-start(), calls=%async_computation.7 | async-start | bytes 1966080 | tf_op jit(solution)/shard_map/reduce_scatter | solution.py:16
  26.8 6.4 slice-start
  26.8 6.4 slice-start.1
  32.2 4.6 copy-start.1
  33.1 7.3 %collective-permute-start = (bf16[512,24,128]{2,0,1:T(8,128)(2,1)S(1)}, bf16[512,24,128]{2,0,1:T(8,128)(2,1)}, u32[]{:S(2)}, u32[]{:S(2)}) collective-permute-start(bf16[512,24,128]{2,0,1:T(8,128)(2,1)S(1)} %bitcast.202), channel_id=1, source_target_pairs={{0,1},{1,0},{2,3},{3,2},{4,5},{5,4},{6,7},{7,6},{8,9},{9,8},{10,11... | collective-permute-start | bytes 9437192 | tf_op jit(solution)/shard_map/ppermute | solution.py:12
  36.7 8.2 %copy-start.12 = (bf16[1,24,2,128,128]{4,3,1,2,0:T(8,128)(2,1)}, bf16[1,24,2,128,128]{4,3,1,2,0:T(8,128)(2,1)S(1)}, u32[]{:S(2)}) copy-start(bf16[1,24,2,128,128]{4,3,1,2,0:T(8,128)(2,1)S(1)} %copy.102) | copy-start | bytes 4718596
  45.0 5.0 copy-start.16
  49.9 4.2 copy-start.6
  49.9 70.6 %collective-permute-start.1 = (bf16[512,24,128]{2,0,1:T(8,128)(2,1)S(1)}, bf16[512,24,128]{2,0,1:T(8,128)(2,1)}, u32[]{:S(2)}, u32[]{:S(2)}) collective-permute-start(bf16[512,24,128]{2,0,1:T(8,128)(2,1)S(1)} %fusion.10), channel_id=1, source_target_pairs={{0,2},{1,3},{2,0},{3,1},{4,6},{5,7},{6,4},{7,5},{8,10},{9,11},{10,... | collective-permute-start | bytes 9437192 | tf_op jit(solution)/shard_map/ppermute | solution.py:12
  50.1 75.0 %copy-start.14 = (bf16[1,24,2,128,128]{4,3,1,2,0:T(8,128)(2,1)}, bf16[1,24,2,128,128]{4,3,1,2,0:T(8,128)(2,1)S(1)}, u32[]{:S(2)}) copy-start(bf16[1,24,2,128,128]{4,3,1,2,0:T(8,128)(2,1)S(1)} %copy.101) | copy-start | bytes 4718596
  131.6 138.2 %collective-permute-start.2 = (bf16[512,24,128]{2,0,1:T(8,128)(2,1)}, bf16[512,24,128]{2,0,1:T(8,128)(2,1)}, u32[]{:S(2)}, u32[]{:S(2)}) collective-permute-start(bf16[512,24,128]{2,0,1:T(8,128)(2,1)} %fusion.11), channel_id=1, source_target_pairs={{0,4},{1,5},{2,6},{3,7},{4,0},{5,1},{6,2},{7,3},{8,12},{9,13},{10,... | collective-permute-start | bytes 9437192 | tf_op jit(solution)/shard_map/ppermute | solution.py:12
  297.4 2.6 copy-start.3
  300.1 135.6 %collective-permute-start.3 = (bf16[512,24,128]{2,0,1:T(8,128)(2,1)}, bf16[512,24,128]{2,0,1:T(8,128)(2,1)}, u32[]{:S(2)}, u32[]{:S(2)}) collective-permute-start(bf16[512,24,128]{2,0,1:T(8,128)(2,1)} %convert_bitcast_fusion.2), channel_id=1, source_target_pairs={{0,4},{1,5},{2,6},{3,7},{4,0},{5,1},{6,2},{7,3},{8,12},{9,13},{10,... | collective-permute-start | bytes 9437192 | tf_op jit(solution)/shard_map/ppermute | solution.py:12
  304.5 4.2 copy-start.4
  304.5 4.7 copy-start.9
  311.9 269.4 %reduce-scatter.8.cloned.1.call-start = ((), (), s32[]{:S(2)}) async-start(), calls=%async_computation.6 | async-start | bytes 1966080 | tf_op jit(solution)/shard_map/reduce_scatter | solution.py:16
  440.3 4.9 copy-start.15
  445.2 5.2 copy-start.5
  445.2 4.2 copy-start.7
  447.8 2.6 copy-start.11
  447.8 70.3 %collective-permute-start.4 = (bf16[512,24,128]{2,0,1:T(8,128)(2,1)}, bf16[512,24,128]{2,0,1:T(8,128)(2,1)}, u32[]{:S(2)}, u32[]{:S(2)}) collective-permute-start(bf16[512,24,128]{2,0,1:T(8,128)(2,1)} %convert_bitcast_fusion.1), channel_id=1, source_target_pairs={{0,2},{1,3},{2,0},{3,1},{4,6},{5,7},{6,4},{7,5},{8,10},{9,11},{10,... | collective-permute-start | bytes 9437192 | tf_op jit(solution)/shard_map/ppermute | solution.py:12
  453.0 129.5 %reduce-scatter.6.cloned.1.call-start = ((), (), s32[]{:S(2)}) async-start(), calls=%async_computation.5 | async-start | bytes 1966080 | tf_op jit(solution)/shard_map/reduce_scatter | solution.py:16
  522.8 4.0 copy-start.2
  526.8 1.6 copy-start.8
  526.8 3.0 copy-start.10
  532.4 89.8 %reduce-scatter.14.cloned.1.call-start = ((), (), s32[]{:S(2)}) async-start(), calls=%async_computation.9 | async-start | bytes 5898240 | tf_op jit(solution)/shard_map/reduce_scatter | solution.py:16
  540.7 141.4 %reduce-scatter.12.cloned.1.call-start = ((), (), s32[]{:S(2)}) async-start(), calls=%async_computation.8 | async-start | bytes 5898240 | tf_op jit(solution)/shard_map/reduce_scatter | solution.py:16
  545.0 5.9 collective-permute-start.5
  560.1 5.7 copy-start.17
  564.1 1.7 copy-start.19
  583.9 2.8 copy-start.20
  (2 other events, 2.1 us)
Sparse Core Ops, SparseCore 0:
  312.0 31.6 reduce-scatter.9
  453.1 31.3 reduce-scatter.7
  532.5 29.8 reduce-scatter.5
  565.2 56.9 reduce-scatter.13
  625.0 56.9 reduce-scatter.11

commit v2 on v1

--- a/solution.py
+++ b/solution.py
@@ -65,6 +65,11 @@
     level_list = [None] * level_count
     for level_index in reversed(range(level_count)):
         weights_now = level_weights[level_index]
+        sent_term = jnp.einsum(
+            "rjd,jcd->rjc", upstream, weights_now[:, 1], preferred_element_type=wide
+        ).astype(jnp.bfloat16)
+        returned = partner(sent_term, "hidden", level_index)
+        sent_term, upstream = lax.optimization_barrier((sent_term, upstream))
         shifted = partner_kept[level_index]
         grad_own = jnp.einsum(
             "rjc,rjd->jcd", inputs_kept[level_index], upstream, preferred_element_type=wide
@@ -75,10 +80,6 @@
         own_term = jnp.einsum(
             "rjd,jcd->rjc", upstream, weights_now[:, 0], preferred_element_type=wide
         )
-        sent_term = jnp.einsum(
-            "rjd,jcd->rjc", upstream, weights_now[:, 1], preferred_element_type=wide
-        ).astype(jnp.bfloat16)
-        returned = partner(sent_term, "hidden", level_index)
         placed = jnp.take(returned, inverse[level_index], axis=1)
         upstream = (own_term + placed.astype(wide)).astype(jnp.bfloat16)
     flat_grad = upstream.reshape(row_count, group_count * block_size)

time: 702 us -> 706 us (level)
  waiting for transfers between devices: 458 us -> 435 us
  other arithmetic: 21 us -> 32.5 us
  starting transfers between devices: 1.01 us -> 11.4 us
    ppermute x6, waiting for transfers between devices: 386 us -> 362 us  [partner(): return lax.ppermute(value, axis, pairs)]
    convert_element_type x1 -> x3, other arithmetic: 4.91 us -> 16.4 us  [local(): upstream = (own_term + placed.astype(wide)).astype(jnp.bfloat16)]
    reduce_scatter x5, starting transfers between devices: 0.78 us -> 11.2 us  [reduce_dp(): lax.psum_scatter(value.astype(jnp.bfloat16), 'dp', scatter_dimension=dim,...]
    gather x4 -> x3, local copies, waits for them, and re-layouts: 18.4 us -> 13.8 us  [local(): placed = jnp.take(returned, inverse[level_index], axis=1)]
  transfers between devices with their start and end apart: 11 -> 11, of which waited for: 7 -> 7; matrix products, arithmetic and copies ran while one was open for 17% -> 20% of each run, Pallas kernels for 0% -> 0%
where the time goes in v2:
time: 706 us; the launch traced here: 696 us
  waiting for transfers between devices  435 us (62%)
  matrix products  111 us (16%)
  local copies, waits for them, and re-layouts  59.6 us (8%)
  other arithmetic  32.5 us (5%)
  blocking collectives  32 us (5%)
  between operations  14.6 us (2%)
  starting transfers between devices  11.4 us (2%)
    ppermute x6, waiting for transfers between devices, partner(): return lax.ppermute(value, axis, pairs)  362 us
    reduce_scatter x5, waiting for transfers between devices, reduce_dp(): lax.psum_scatter(value.astype(jnp.bfloat16), 'dp', scatter_dimension=dim,...  73.4 us
    dot_general x3, matrix products, local(): jnp.einsum('rjc,jcd->rjd', shifted, weights_now[:, 1], preferred_element_...  18.8 us
    psum x1, blocking collectives, local(): sum_squares = lax.psum(jnp.sum(tokens_wide * tokens_wide, axis=1), 'hidden')  18.1 us
    dot_general x3, matrix products, local(): jnp.einsum('rjd,jcd->rjc', upstream, weights_now[:, 0], preferred_element...  16.7 us
    convert_element_type x3, other arithmetic, local(): upstream = (own_term + placed.astype(wide)).astype(jnp.bfloat16)  16.4 us
  transfers between devices with their start and end apart: 11, of which 7 were waited for; matrix products, arithmetic and copies ran while one was open for 20% of the time, Pallas kernels for 0%

profile of v2, /device:TPU:0, one launch (start us, length us, event | category | flops | bytes accessed | tf_op | source)
XLA Modules:
  0.0 696.0 jit_solution(6621223480015611818)
XLA Ops:
  8.7 18.1 %psum.14 = f32[512]{0:T(512)S(1)} all-reduce(f32[512]{0:T(512)S(1)} %fusion.48), channel_id=1, replica_groups=mesh['dp'=4,'hidden'=8] {'hidden'}, use_global_device_ids=true, to_apply=%region_1.0 | all-reduce | flops 512 | bytes 4096 | tf_op jit(solution)/shard_map/psum | solution.py:28
  26.8 5.4 fusion.41
  40.4 4.6 gather_fusion
  45.0 4.9 fusion.10
  54.2 66.4 %collective-permute-done.1 = bf16[512,24,128]{2,0,1:T(8,128)(2,1)} collective-permute-done((bf16[512,24,128]{2,0,1:T(8,128)(2,1)S(1)}, bf16[512,24,128]{2,0,1:T(8,128)(2,1)}, u32[]{:S(2)}, u32[]{:S(2)}) %collective-permute-start.1) | collective-permute-done | bytes 3145760 | tf_op jit(solution)/shard_map/ppermute | solution.py:12
  120.6 4.6 gather_fusion.1
  125.2 6.5 fusion.11
  133.7 5.6 fusion.84
  139.2 130.7 %collective-permute-done.2 = bf16[512,24,128]{2,0,1:T(8,128)(2,1)} collective-permute-done((bf16[512,24,128]{2,0,1:T(8,128)(2,1)}, bf16[512,24,128]{2,0,1:T(8,128)(2,1)}, u32[]{:S(2)}, u32[]{:S(2)}) %collective-permute-start.2) | collective-permute-done | bytes 3145760 | tf_op jit(solution)/shard_map/ppermute | solution.py:12
  269.9 4.7 gather_fusion.2
  274.6 7.5 %fusion.12 = f32[24,512,128]{1,2,0:T(8,128)} fusion(f32[24,512,128]{1,2,0:T(8,128)} %fusion.84, bf16[24,512,128]{2,1,0:T(8,128)(2,1)} %gather_fusion.2, pred[24]{0:T(512)(128)(4,1)S(1)} %get-tuple-element.28, bf16[24,2,128,128]{2,3,0,1:T(8,128)(2,1)S(1)} %bitcast.182), kind=kOutput, calls=%fused_computation.31 | convolution fusion | flops 408944640 | bytes 16515584 | tf_op jit(solution)/shard_map/rjc,jcd->rjd/dot_general | solution.py:48
  282.1 6.9 copy.44
  289.0 8.6 %fusion.6 = bf16[512,3072]{1,0:T(8,128)(2,1)S(1)} fusion(f32[512,3072]{1,0:T(8,128)} %copy.44, bf16[512,768]{1,0:T(8,128)(2,1)S(1)} %copy-done, bf16[3072,768]{1,0:T(8,128)(2,1)} %param.12), kind=kOutput, calls=%fused_computation.15 | convolution fusion | flops 2447376384 | bytes 14942208 | tf_op jit(solution)/shard_map/rd,fd->rf/dot_general | solution.py:60
  314.9 10.8 %reduce-scatter.8.cloned.1.call-start = ((), (), s32[]{:S(2)}) async-start(), calls=%async_computation.6 | async-start | bytes 1966080 | tf_op jit(solution)/shard_map/reduce_scatter | solution.py:16
  325.7 5.6 fusion.33
  331.3 104.5 %collective-permute-done.3 = bf16[512,24,128]{2,0,1:T(8,128)(2,1)} collective-permute-done((bf16[512,24,128]{2,0,1:T(8,128)(2,1)}, bf16[512,24,128]{2,0,1:T(8,128)(2,1)}, u32[]{:S(2)}, u32[]{:S(2)}) %collective-permute-start.3) | collective-permute-done | bytes 3145760 | tf_op jit(solution)/shard_map/ppermute | solution.py:12
  435.8 4.6 gather_fusion.3
  440.4 4.9 fusion.9
  453.2 5.5 fusion.82
  458.7 59.7 %collective-permute-done.4 = bf16[512,24,128]{2,0,1:T(8,128)(2,1)} collective-permute-done((bf16[512,24,128]{2,0,1:T(8,128)(2,1)}, bf16[512,24,128]{2,0,1:T(8,128)(2,1)}, u32[]{:S(2)}, u32[]{:S(2)}) %collective-permute-start.4) | collective-permute-done | bytes 3145760 | tf_op jit(solution)/shard_map/ppermute | solution.py:12
  522.9 4.9 fusion.8
  536.5 8.2 %convolution_convert_fusion = bf16[3072,768]{1,0:T(8,128)(2,1)} fusion(bf16[512,768]{1,0:T(8,128)(2,1)S(1)} %copy-done, f32[512,3072]{1,0:T(8,128)} %copy.44), kind=kOutput, calls=%fused_computation.26 | convolution fusion | flops 2432434176 | bytes 11796480 | tf_op jit(solution)/shard_map/rf,rd->fd/dot_general | solution.py:58
  545.1 5.6 fusion.80
  551.0 4.6 gather_fusion.5
  555.6 6.6 fusion.7
  562.3 4.7 copy.51
  567.0 6.5 convolution_convert_fusion.1
  573.5 9.5 %convolution_convert_fusion.5 = bf16[512,768]{1,0:T(8,128)(2,1)} fusion(bf16[3072,768]{1,0:T(8,128)(2,1)} %param.12, f32[512,3072]{1,0:T(8,128)} %copy.44), kind=kOutput, calls=%fused_computation.85 | convolution fusion | flops 2430468096 | bytes 11796480 | tf_op jit(solution)/shard_map/dot_general | solution.py:56
  589.5 5.2 fusion.49
  594.7 13.9 %psum.15 = f32[512]{0:T(512)S(1)} all-reduce(f32[512]{0:T(512)S(1)} %get-tuple-element.45), channel_id=1, replica_groups=mesh['dp'=4,'hidden'=8] {'hidden'}, use_global_device_ids=true, to_apply=%region_4.6 | all-reduce | flops 512 | bytes 4096 | tf_op jit(solution)/shard_map/psum | solution.py:90
  609.9 16.4 %reduce-scatter.14.cloned.1.call-done = bf16[768,768]{1,0:T(8,128)(2,1)} async-done(((bf16[3072,768]{1,0:T(8,128)(2,1)}), bf16[768,768]{1,0:T(8,128)(2,1)}) %reduce-scatter.14.cloned.1.call-update) | async-done | bytes 1179664 | tf_op jit(solution)/shard_map/reduce_scatter | solution.py:16
  629.2 56.9 %reduce-scatter.12.cloned.1.call-done = bf16[192,3072]{1,0:T(8,128)(2,1)} async-done(((bf16[768,3072]{1,0:T(8,128)(2,1)}), bf16[192,3072]{1,0:T(8,128)(2,1)}) %reduce-scatter.12.cloned.1.call-update) | async-done | bytes 1179664 | tf_op jit(solution)/shard_map/reduce_scatter | solution.py:16
  (111 shorter events, 68.3 us)
Async XLA Ops:
  7.2 281.8 %copy-start = (bf16[512,768]{1,0:T(8,128)(2,1)S(1)}, bf16[512,768]{1,0:T(8,128)(2,1)}, u32[]{:S(2)}) copy-start(bf16[512,768]{1,0:T(8,128)(2,1)} %param.9) | copy-start | bytes 2359300
  7.2 575.9 %reduce-scatter.10.cloned.1.call-start = ((), (), s32[]{:S(2)}) async-start(), calls=%async_computation.7 | async-start | bytes 1966080 | tf_op jit(solution)/shard_map/reduce_scatter | solution.py:16
  26.8 6.4 slice-start
  26.8 6.4 slice-start.1
  32.2 4.6 copy-start.3
  33.1 7.4 %collective-permute-start = (bf16[512,24,128]{2,0,1:T(8,128)(2,1)S(1)}, bf16[512,24,128]{2,0,1:T(8,128)(2,1)}, u32[]{:S(2)}, u32[]{:S(2)}) collective-permute-start(bf16[512,24,128]{2,0,1:T(8,128)(2,1)S(1)} %bitcast.198), channel_id=1, source_target_pairs={{0,1},{1,0},{2,3},{3,2},{4,5},{5,4},{6,7},{7,6},{8,9},{9,8},{10,11... | collective-permute-start | bytes 9437192 | tf_op jit(solution)/shard_map/ppermute | solution.py:12
  36.7 8.3 %copy-start.8 = (bf16[1,24,2,128,128]{4,3,1,2,0:T(8,128)(2,1)}, bf16[1,24,2,128,128]{4,3,1,2,0:T(8,128)(2,1)S(1)}, u32[]{:S(2)}) copy-start(bf16[1,24,2,128,128]{4,3,1,2,0:T(8,128)(2,1)S(1)} %copy.102) | copy-start | bytes 4718596
  45.0 5.0 copy-start.16
  49.9 4.3 copy-start.6
  49.9 70.6 %collective-permute-start.1 = (bf16[512,24,128]{2,0,1:T(8,128)(2,1)S(1)}, bf16[512,24,128]{2,0,1:T(8,128)(2,1)}, u32[]{:S(2)}, u32[]{:S(2)}) collective-permute-start(bf16[512,24,128]{2,0,1:T(8,128)(2,1)S(1)} %fusion.10), channel_id=1, source_target_pairs={{0,2},{1,3},{2,0},{3,1},{4,6},{5,7},{6,4},{7,5},{8,10},{9,11},{10,... | collective-permute-start | bytes 9437192 | tf_op jit(solution)/shard_map/ppermute | solution.py:12
  50.1 75.1 %copy-start.10 = (bf16[1,24,2,128,128]{4,3,1,2,0:T(8,128)(2,1)}, bf16[1,24,2,128,128]{4,3,1,2,0:T(8,128)(2,1)S(1)}, u32[]{:S(2)}) copy-start(bf16[1,24,2,128,128]{4,3,1,2,0:T(8,128)(2,1)S(1)} %copy.101) | copy-start | bytes 4718596
  131.7 138.2 %collective-permute-start.2 = (bf16[512,24,128]{2,0,1:T(8,128)(2,1)}, bf16[512,24,128]{2,0,1:T(8,128)(2,1)}, u32[]{:S(2)}, u32[]{:S(2)}) collective-permute-start(bf16[512,24,128]{2,0,1:T(8,128)(2,1)} %fusion.11), channel_id=1, source_target_pairs={{0,4},{1,5},{2,6},{3,7},{4,0},{5,1},{6,2},{7,3},{8,12},{9,13},{10,... | collective-permute-start | bytes 9437192 | tf_op jit(solution)/shard_map/ppermute | solution.py:12
  297.6 2.7 copy-start.13
  300.2 135.6 %collective-permute-start.3 = (bf16[512,24,128]{2,0,1:T(8,128)(2,1)}, bf16[512,24,128]{2,0,1:T(8,128)(2,1)}, u32[]{:S(2)}, u32[]{:S(2)}) collective-permute-start(bf16[512,24,128]{2,0,1:T(8,128)(2,1)} %convert_bitcast_fusion.2), channel_id=1, source_target_pairs={{0,4},{1,5},{2,6},{3,7},{4,0},{5,1},{6,2},{7,3},{8,12},{9,13},{10,... | collective-permute-start | bytes 9437192 | tf_op jit(solution)/shard_map/ppermute | solution.py:12
  307.4 4.5 copy-start.5
  307.4 4.5 copy-start.12
  314.9 269.3 %reduce-scatter.8.cloned.1.call-start = ((), (), s32[]{:S(2)}) async-start(), calls=%async_computation.6 | async-start | bytes 1966080 | tf_op jit(solution)/shard_map/reduce_scatter | solution.py:16
  440.4 4.9 copy-start.11
  445.4 5.2 copy-start.2
  445.4 4.2 copy-start.7
  448.0 2.6 copy-start.15
  448.0 70.3 %collective-permute-start.4 = (bf16[512,24,128]{2,0,1:T(8,128)(2,1)}, bf16[512,24,128]{2,0,1:T(8,128)(2,1)}, u32[]{:S(2)}, u32[]{:S(2)}) collective-permute-start(bf16[512,24,128]{2,0,1:T(8,128)(2,1)} %convert_bitcast_fusion.1), channel_id=1, source_target_pairs={{0,2},{1,3},{2,0},{3,1},{4,6},{5,7},{6,4},{7,5},{8,10},{9,11},{10,... | collective-permute-start | bytes 9437192 | tf_op jit(solution)/shard_map/ppermute | solution.py:12
  453.1 132.2 %reduce-scatter.6.cloned.1.call-start = ((), (), s32[]{:S(2)}) async-start(), calls=%async_computation.5 | async-start | bytes 1966080 | tf_op jit(solution)/shard_map/reduce_scatter | solution.py:16
  522.9 4.9 copy-start.9
  527.8 5.3 copy-start.1
  527.8 4.2 copy-start.4
  532.0 1.9 copy-start.14
  536.4 89.9 %reduce-scatter.14.cloned.1.call-start = ((), (), s32[]{:S(2)}) async-start(), calls=%async_computation.9 | async-start | bytes 5898240 | tf_op jit(solution)/shard_map/reduce_scatter | solution.py:16
  544.7 141.4 %reduce-scatter.12.cloned.1.call-start = ((), (), s32[]{:S(2)}) async-start(), calls=%async_computation.8 | async-start | bytes 5898240 | tf_op jit(solution)/shard_map/reduce_scatter | solution.py:16
  545.0 6.1 collective-permute-start.5
  562.3 4.7 copy-start.18
  586.7 2.8 copy-start.17
  (1 other events, 0.7 us)
Sparse Core Ops, SparseCore 0:
  315.0 31.6 reduce-scatter.9
  453.3 31.4 reduce-scatter.7
  536.5 29.8 reduce-scatter.5
  569.3 56.9 reduce-scatter.13
  629.1 56.9 reduce-scatter.11
